TPU v7x, 32 devices: a whole 2x2x4 slice. The times are simulated.
32 devices in a mesh: row: 4 (over y, x), col: 8 (over z, core).
Axes of the slice: x: 2, y: 2, z: 4, core: 2. Of those that a mesh axis runs over, the one named last changes fastest.
Arguments:
- features: bfloat16 [8192, 128], P(('row', 'col')), may hold values from -6 to 6
- weight: bfloat16 [128, 256], replicated, may hold values from -0.5 to 0.5
- cotangent: bfloat16 [8192, 256], P(('row', 'col')), may hold values from -6 to 6
- tile_values: bfloat16 [4, 8, 96, 128, 128], P('row', 'col'), may hold values from -0.3125 to 0.3125
- tile_rows: int32 [4, 8, 96], P('row', 'col'), may hold values from 0 to 15
- tile_cols: int32 [4, 8, 96], P('row', 'col'), may hold values from 0 to 7
- tile_counts: int32 [4, 8], P('row', 'col'), may hold values from 12 to 96, as said below
Outputs:
- output: bfloat16 [8192, 256], P(('row', 'col'))
- grad_features: bfloat16 [8192, 128], P(('row', 'col'))
- grad_weight: float32 [128, 256], replicated
Inputs may be any that keep to these rules, and one draw needn't show every extreme that they name: Slots 0 to tile_counts - 1 of a grid cell are live and the rest are ignored; the (row tile, column tile) pairs of a cell's live slots are distinct; some cells hold 96 live slots.
All inputs are finite; a program needn't handle non-finite values.
Results may differ from a plain program's by a relative error of at most 0.0049.
Values may be sent and summed in bfloat16 or wider, within the bound.
A program may use at most 128 MiB of HBM per device.

v0:
```python
import functools

import jax
import jax.numpy as jnp
from jax import lax
from jax.experimental import pallas as pl
from jax.experimental.pallas import tpu as pltpu
from jax.sharding import PartitionSpec as P

MESH = pl.DeviceIdType.MESH


def dot(a, b):
    return jnp.dot(a, b, preferred_element_type=jnp.float32)


def split_high_low(values):
    high = values.astype(jnp.bfloat16)
    return high, (values - high.astype(jnp.float32)).astype(jnp.bfloat16)


def finish(*refs):
    count = len(refs) // 2
    for source, result in zip(refs[:count], refs[count:]):
        result[...] = source[...]


def kernel(rows, cols, sizes, live_count, tile_row, tile_col, feats, weight, cot, tiles, out, grad_feat, grad_weight,
           keys, table, slot_of, summing, slots, dense, flipped, feat_all, pair_send, pair_recv, pair_own, hop_send, hop_recv,
           grad_all, acc, row_send, row_recv, w_term, w_row, w_quarter, w_pair, w_hop, w_all,
           load_sem, feat_s, feat_r, pair_s, pair_r, hop_s, hop_r, gp_s, gp_r, gz_s, gz_r, gf_s, gf_r,
           row_s, row_r, w1_s, w1_r, w2_s, w2_r, w3_s, w3_r, w4_s, w4_r):
    block, tile, row_tiles, col_tiles, slot_total = sizes
    chips = cols // 2
    i = lax.axis_index("row")
    j = lax.axis_index("col")
    q = j // 2
    core = j % 2
    other = 1 - core
    partner = (i, 2 * q + other)

    def row_at(step):
        return lax.rem(i + step, rows)

    def chip_at(step):
        if chips & (chips - 1):
            return lax.rem(chips + step - q, chips)
        paired, bit = q, 1
        while bit <= step:
            if step & bit:
                paired = paired + bit - 2 * bit * ((q // bit) % 2)
            bit *= 2
        return paired

    def send(src, dst, ssem, rsem, device):
        copy = pltpu.make_async_remote_copy(
            src_ref=src, dst_ref=dst, send_sem=ssem, recv_sem=rsem, device_id=device, device_id_type=MESH)
        copy.start()
        return copy

    started = []

    load_tiles = pltpu.make_async_copy(tiles, slots.at[pl.ds(0, slot_total)], load_sem.at[0])
    load_tiles.start()
    own_block = pl.ds(pl.multiple_of(i * block, block), block)
    load_feats = pltpu.make_async_copy(feats, feat_all.at[own_block], load_sem.at[1])
    load_feats.start()

    barrier = pltpu.get_barrier_semaphore()
    peers = [partner]
    for d in range(1, rows):
        peers.append((row_at(d), j))
        peers.append((row_at(d), 2 * q + other))
    for d in range(1, chips):
        peers.append((i, 2 * chip_at(d) + core))
    for peer in peers:
        pl.semaphore_signal(barrier, inc=1, device_id=peer, device_id_type=MESH)

    cell_total = row_tiles * col_tiles
    lanes = lax.broadcasted_iota(jnp.int32, (1, slot_total), 1)
    keys[...] = jnp.full(keys.shape, -1, jnp.int32)
    keys[:, :slot_total] = jnp.where(lanes < live_count[0, 0], tile_row[...] * col_tiles + tile_col[...], -1)
    padded = keys.shape[1]
    key_columns = jnp.broadcast_to(keys[...], (128, padded)).T
    slot_ids = lax.broadcasted_iota(jnp.int32, (padded, 128), 0) - slot_total
    cell_ids = lax.broadcasted_iota(jnp.int32, (padded, 128), 1)
    for first in range(0, cell_total, 128):
        found = jnp.where(key_columns == cell_ids + first, slot_ids, 0)
        table[:, first:first + 128] = jnp.sum(found, axis=0, keepdims=True) + slot_total
    load_table = pltpu.make_async_copy(table, slot_of, load_sem.at[2])
    load_table.start()
    slots[slot_total] = jnp.zeros((tile, tile), jnp.bfloat16)
    pl.semaphore_wait(barrier, len(peers))

    feat_copies = []
    for d in range(1, rows):
        feat_copies.append(send(feats, feat_all.at[own_block], feat_s.at[d - 1], feat_r.at[d - 1], (row_at(d), j)))

    load_table.wait()
    load_tiles.wait()

    def place(r, carry):
        at = pl.ds(pl.multiple_of(r * tile, tile), tile)
        for c in range(col_tiles):
            dense[at, c * tile:(c + 1) * tile] = slots[slot_of[0, r * col_tiles + c]]
        return carry

    lax.fori_loop(0, row_tiles, place, 0)

    def product_at(at, source):
        source_at = pl.ds(pl.multiple_of(source * block, block), block)
        return dot(dense[at, source_at], feat_all[source_at, :])

    load_feats.wait()
    for d in range(rows - 1):
        if d:
            feat_copies[d - 1].wait_recv()
        source = lax.rem(i - d + rows, rows)

        def add_source(dest, carry):
            at = pl.ds(pl.multiple_of(dest * block, block), block)
            if d:
                summing[at, :] += product_at(at, source)
            else:
                summing[at, :] = product_at(at, source)
            return carry

        lax.fori_loop(0, cols, add_source, 0)
    feat_copies[rows - 2].wait_recv()
    last = lax.rem(i + 1, rows)

    def partial_of(dest):
        at = pl.ds(pl.multiple_of(dest * block, block), block)
        return summing[at, :] + product_at(at, last)

    started += feat_copies
    order = list(range(chips - 1, -1, -1))
    pair_copies = {}
    for d in order:
        pair_send[d] = partial_of(2 * chip_at(d) + other).astype(jnp.bfloat16)
        pair_copies[d] = send(pair_send.at[d], pair_recv.at[d], pair_s.at[d], pair_r.at[d], partner)
    hop_copies = {}
    for d in order:
        mine = partial_of(2 * chip_at(d) + core)
        pair_copies[d].wait_recv()
        mine = mine + pair_recv[d].astype(jnp.float32)
        if d:
            hop_send[d - 1] = mine.astype(jnp.bfloat16)
            hop_copies[d] = send(hop_send.at[d - 1], hop_recv.at[d - 1], hop_s.at[d - 1], hop_r.at[d - 1],
                                 (i, 2 * chip_at(d) + core))
        else:
            pair_own[...] = mine
    started += list(pair_copies.values()) + list(hop_copies.values())

    def turn(r, carry):
        at = pl.ds(pl.multiple_of(r * tile, tile), tile)
        for c in range(col_tiles):
            flipped[c * tile:(c + 1) * tile, at] = dense[at, c * tile:(c + 1) * tile].T
        return carry

    lax.fori_loop(0, row_tiles, turn, 0)

    mixed = pair_own[...]
    for d in range(1, chips):
        hop_copies[d].wait_recv()
        mixed = mixed + hop_recv[d - 1].astype(jnp.float32)

    w = weight[...]
    high, low = split_high_low(mixed)
    summed = dot(high, w) + dot(low, w)
    gate = 1.0 / (1.0 + jnp.exp(-summed))
    slope = gate * (1.0 + summed * (1.0 - gate))
    grad = (cot[...].astype(jnp.float32) * slope).astype(jnp.bfloat16)
    grad_all[j] = lax.dot_general(
        grad, w, (((1,), (1,)), ((), ())), preferred_element_type=jnp.float32).astype(jnp.bfloat16)
    gz_copies = {}
    for d in order[:-1]:
        gz_copies[d] = send(grad_all.at[j], grad_all.at[j], gz_s.at[d - 1], gz_r.at[d - 1],
                            (i, 2 * chip_at(d) + core))
    gp_copy = send(grad_all.at[j], grad_all.at[j], gp_s.at[0], gp_r.at[0], partner)
    out[...] = (summed * gate).astype(out.dtype)

    mixed_t = mixed.T
    high_t, low_t = split_high_low(mixed_t)
    scale = float(rows * cols * block) ** -0.5
    w_term[...] = (dot(high_t, grad) + dot(low_t, grad)) * scale
    quarter = w_term.shape[0] // rows
    half = quarter // 2

    def quarter_at(index):
        return pl.ds(pl.multiple_of(index * quarter, quarter), quarter)

    w1_copies = []
    for d in range(1, rows):
        w1_copies.append(send(w_term.at[quarter_at(row_at(d))], w_row.at[d - 1], w1_s.at[d - 1], w1_r.at[d - 1],
                              (row_at(d), j)))

    def add_block(source, first):
        term = dot(flipped[:, pl.ds(pl.multiple_of(source * block, block), block)], grad_all[source])
        if first:
            acc[...] = term
        else:
            acc[...] += term

    add_block(j, True)
    gp_copy.wait_recv()
    add_block(2 * q + other, False)

    total = w_term[quarter_at(i)]
    for d, copy in enumerate(w1_copies):
        copy.wait_recv()
        total = total + w_row[d]
    w_quarter[...] = total
    w2_copy = send(w_quarter.at[pl.ds(pl.multiple_of(other * half, half), half)], w_pair, w2_s.at[0], w2_r.at[0],
                   partner)
    started += list(gz_copies.values()) + [gp_copy] + w1_copies + [w2_copy]

    gf_copies = []
    w3_copies = []

    def second_weight_step():
        w2_copy.wait_recv()
        w_hop[q] = w_quarter[pl.ds(pl.multiple_of(core * half, half), half)] + w_pair[...]
        for d in range(1, chips):
            w3_copies.append(send(w_hop.at[q], w_hop.at[q], w3_s.at[d - 1], w3_r.at[d - 1],
                                  (i, 2 * chip_at(d) + core)))

    for d in range(1, chips):
        source = chip_at(d)
        gz_copies[d].wait_recv()
        source_at = 2 * source + core
        gf_copies.append(send(grad_all.at[source_at], grad_all.at[source_at], gf_s.at[d - 1], gf_r.at[d - 1],
                              partner))
        add_block(source_at, False)
        if d == 1:
            second_weight_step()
        gf_copies[d - 1].wait_recv()
        add_block(2 * source + other, False)
    started += gf_copies + w3_copies

    row_copies = []
    for d in range(1, rows):
        at = pl.ds(pl.multiple_of(row_at(d) * block, block), block)
        row_send[d - 1] = acc[at, :].astype(jnp.bfloat16)
        row_copies.append(send(row_send.at[d - 1], row_recv.at[d - 1], row_s.at[d - 1], row_r.at[d - 1],
                               (row_at(d), j)))
    started += row_copies

    for copy in w3_copies:
        copy.wait_recv()
    piece = w_hop[0]
    for k in range(1, chips):
        piece = piece + w_hop[k]
    mine_at = 2 * i + core
    w_all[mine_at] = piece
    w4_copies = []
    for d in range(1, 2 * rows):
        target = (row_at(d // 2), 2 * q + (core if d % 2 == 0 else other))
        w4_copies.append(send(w_all.at[mine_at], w_all.at[mine_at], w4_s.at[d - 1], w4_r.at[d - 1], target))
    started += w4_copies

    final = acc[own_block, :]
    for d, copy in enumerate(row_copies):
        copy.wait_recv()
        final = final + row_recv[d].astype(jnp.float32)
    grad_feat[...] = final.astype(grad_feat.dtype)

    for copy in w4_copies:
        copy.wait_recv()
    grad_weight[...] = w_all[...].reshape(grad_weight.shape)
    for copy in started:
        copy.wait_send()


def local(features, weight, cotangent, tile_values, tile_rows, tile_cols, tile_counts):
    rows = lax.axis_size("row")
    cols = lax.axis_size("col")
    chips = cols // 2
    block, width = features.shape
    hidden = weight.shape[1]
    slot_total, tile = tile_values.shape[2], tile_values.shape[3]
    row_tiles = cols * block // tile
    col_tiles = rows * block // tile
    cell_total = row_tiles * col_tiles
    half = width // rows // 2
    bf16, f32 = jnp.bfloat16, jnp.float32
    dma = pltpu.SemaphoreType.DMA
    v, any_space = pltpu.VMEM, pl.ANY
    sizes = (block, tile, row_tiles, col_tiles, slot_total)
    scratch = [
        v((1, pl.cdiv(slot_total, 128) * 128), jnp.int32),
        v((1, cell_total), jnp.int32),
        pltpu.SMEM((1, cell_total), jnp.int32),
        v((row_tiles * tile, width), f32),
        v((slot_total + 1, tile, tile), bf16),
        v((row_tiles * tile, col_tiles * tile), bf16),
        v((col_tiles * tile, row_tiles * tile), bf16),
        v((rows * block, width), bf16),
        v((chips, block, width), bf16),
        v((chips, block, width), bf16),
        v((block, width), f32),
        v((chips - 1, block, width), bf16),
        v((chips - 1, block, width), bf16),
        v((cols, block, width), bf16),
        v((rows * block, width), f32),
        v((rows - 1, block, width), bf16),
        v((rows - 1, block, width), bf16),
        v((width, hidden), f32),
        v((rows - 1, 2 * half, hidden), f32),
        v((2 * half, hidden), f32),
        v((half, hidden), f32),
        v((chips, half, hidden), f32),
        v((2 * rows, half, hidden), f32),
        dma((3,)),
    ]
    for count in (rows - 1, chips, chips - 1, 1, chips - 1, chips - 1, rows - 1, rows - 1, 1, chips - 1,
                  2 * rows - 1):
        scratch += [dma((count,)), dma((count,))]
    vmem = pl.BlockSpec(memory_space=pltpu.VMEM)
    hbm = pl.BlockSpec(memory_space=any_space)
    results = (
        jax.ShapeDtypeStruct((block, hidden), bf16),
        jax.ShapeDtypeStruct((block, width), bf16),
        jax.ShapeDtypeStruct((width, hidden), f32),
    )
    values = pl.pallas_call(
        functools.partial(kernel, rows, cols, sizes),
        out_shape=results,
        in_specs=[pl.BlockSpec(memory_space=pltpu.SMEM), vmem, vmem, hbm, vmem, vmem, hbm],
        out_specs=(vmem, vmem, vmem),
        scratch_shapes=scratch,
        compiler_params=pltpu.CompilerParams(collective_id=0, has_side_effects=True),
    )(tile_counts, tile_rows[0], tile_cols[0], features, weight, cotangent, tile_values[0, 0])
    return pl.pallas_call(
        finish,
        out_shape=results,
        in_specs=[vmem] * 3,
        out_specs=(vmem, vmem, vmem),
    )(*values)


def solution(mesh):
    placed = (
        P(("row", "col"), None),
        P(),
        P(("row", "col"), None),
        P("row", "col", None, None, None),
        P("row", "col", None),
        P("row", "col", None),
        P("row", "col"),
    )
    return jax.shard_map(
        local,
        mesh=mesh,
        in_specs=placed,
        out_specs=(P(("row", "col"), None), P(("row", "col"), None), P()),
        check_vma=False,
    )
```

profile of v0, /device:TPU:0, one launch (start us, length us, event | category | flops | bytes accessed | tf_op | source)
XLA Modules:
  0.0 42.0 jit_solution(12754825871713404532)
XLA Ops:
  1.3 39.0 %shard_map.94 = (bf16[256,256]{1,0:T(8,128)(2,1)}, bf16[256,128]{1,0:T(8,128)(2,1)}, f32[128,256]{1,0:T(8,128)}) custom-call(s32[1,1]{1,0:T(1,128)S(6)} %copy.10.live_count, s32[1,96]{1,0:T(1,128)} %bitcast.4, s32[1,96]{1,0:T(1,128)} %bitcast.5, bf16[256,128]{1,0:T(8,128)(2,1)} %feats.1, bf16[128,256]{1,0:T(8,128)(2,1)} %weight.1, bf16[256,256]{1,0:T(8,128)(2,1)} %cot.1, ...), custom_call_target="tpu_custom_call" | custom-call | tf_op jit(solution)/shard_map/pallas_call | solution.py:326
  40.3 1.7 %shard_map.95 = (bf16[256,256]{1,0:T(8,128)(2,1)}, bf16[256,128]{1,0:T(8,128)(2,1)}, f32[128,256]{1,0:T(8,128)}) custom-call(bf16[256,256]{1,0:T(8,128)(2,1)} %get-tuple-element.6.refs_0_, bf16[256,128]{1,0:T(8,128)(2,1)} %get-tuple-element.7.refs_1_, f32[128,256]{1,0:T(8,128)} %get-tuple-element.8.refs_2_), custom_call_target="tpu_custom_call" | custom-call | tf_op jit(solution)/shard_map/pallas_call | solution.py:334
where the time goes:
time: 42.2 us; the launch traced here: 42 us
  Pallas kernels  40.8 us (97%)
  between operations  1.29 us (3%)
    pallas_call x1, Pallas kernels, local(): pl.pallas_call(functools.partial(kernel, rows, cols, sizes), out_shape=re...  39 us
    pallas_call x1, Pallas kernels, local(): pl.pallas_call(finish, out_shape=results, in_specs=[vmem] * 3, out_specs=...  1.73 us

commit v1 on v0

v1 whole, which is shorter than its diff:
```python
import functools

import jax
import jax.numpy as jnp
from jax import lax
from jax.experimental import pallas as pl
from jax.experimental.pallas import tpu as pltpu
from jax.sharding import PartitionSpec as P

MESH = pl.DeviceIdType.MESH
PARTS = 2


def dot_nn(a, b):
    return lax.dot_general(a, b, (((1,), (0,)), ((), ())), preferred_element_type=jnp.float32)


def dot_nt(a, b):
    return lax.dot_general(a, b, (((1,), (1,)), ((), ())), preferred_element_type=jnp.float32)


def split_high_low(values):
    high = values.astype(jnp.bfloat16)
    return high, (values - high.astype(jnp.float32)).astype(jnp.bfloat16)


def finish(*refs):
    count = len(refs) // 2
    sems = refs[-1]
    copies = [pltpu.make_async_copy(refs[k], refs[count + k], sems.at[k]) for k in range(count)]
    for copy in copies:
        copy.start()
    for copy in copies:
        copy.wait()


def partner_index(index, step, count):
    if count & (count - 1):
        return lax.rem(count + step - index, count)
    paired, bit = index, 1
    while bit <= step:
        if step & bit:
            paired = paired + bit - 2 * bit * ((index // bit) % 2)
        bit *= 2
    return paired


def each(count, body):
    if count <= 8:
        for index in range(count):
            body(index)
    else:
        lax.fori_loop(0, count, lambda index, carry: (body(index), carry)[1], 0)


def kernel(rows, cols, sizes, live_hbm, row_hbm, col_hbm, feats_hbm, weight_hbm, cot_hbm, tiles_hbm,
           out, grad_feat, grad_weight,
           live, tile_row, tile_col, feats, weight, cot, keys, table, slot_of, slots, dense, weight_t, cot_t,
           feat_all, part, pair_send, pair_recv, own_sum, hop_send, hop_recv, grad_all, acc, row_send, row_recv,
           w_term, w_row, w_quarter, w_pair, w_hop, w_all,
           load_sem, feat_s, feat_r, pair_s, pair_r, hop_s, hop_r, gp_s, gp_r, gz_s, gz_r, gf_s, gf_r,
           row_s, row_r, w1_s, w1_r, w2_s, w2_r, w3_s, w3_r, w4_s, w4_r, w5_s, w5_r):
    block, tile, row_tiles, col_tiles, slot_total = sizes
    chips = cols // 2
    width = feats.shape[1]
    piece = width // PARTS
    i = lax.axis_index("row")
    j = lax.axis_index("col")
    q = j // 2
    core = j % 2
    other = 1 - core
    partner = (i, 2 * q + other)
    f32, bf16 = jnp.float32, jnp.bfloat16

    def row_at(step):
        return partner_index(i, step, rows)

    def chip_at(step):
        return partner_index(q, step, chips)

    def row_peer(step):
        return (row_at(step), j)

    def chip_peer(step):
        return (i, 2 * chip_at(step) + core)

    started = []

    def send(src, dst, ssem, rsem, device):
        copy = pltpu.make_async_remote_copy(
            src_ref=src, dst_ref=dst, send_sem=ssem, recv_sem=rsem, device_id=device, device_id_type=MESH)
        copy.start()
        started.append(copy)
        return copy

    barrier = pltpu.get_barrier_semaphore()
    peers = [partner] + [row_peer(d) for d in range(1, rows)] + [chip_peer(d) for d in range(1, chips)]
    for peer in peers:
        pl.semaphore_signal(barrier, inc=1, device_id=peer, device_id_type=MESH)

    loads = []
    for k, (src, dst) in enumerate((
            (live_hbm, live), (row_hbm, tile_row), (col_hbm, tile_col), (feats_hbm, feats),
            (tiles_hbm, slots.at[pl.ds(0, slot_total)]), (weight_hbm, weight), (cot_hbm, cot))):
        loads.append(pltpu.make_async_copy(src, dst, load_sem.at[k]))
        loads[-1].start()
    slots[slot_total] = jnp.zeros((tile, tile), bf16)
    keys[...] = jnp.full(keys.shape, -1, jnp.int32)

    for copy in loads[:3]:
        copy.wait()
    cell_total = row_tiles * col_tiles
    lanes = lax.broadcasted_iota(jnp.int32, (1, slot_total), 1)
    keys[:, :slot_total] = jnp.where(lanes < live[...], tile_row[...] * col_tiles + tile_col[...], -1)
    padded = keys.shape[1]
    key_columns = jnp.broadcast_to(keys[...], (128, padded)).T
    slot_ids = lax.broadcasted_iota(jnp.int32, (padded, 128), 0) - slot_total
    cell_ids = lax.broadcasted_iota(jnp.int32, (padded, 128), 1)
    for first in range(0, cell_total, 128):
        found = jnp.where(key_columns == cell_ids + first, slot_ids, 0)
        table[:, first:first + 128] = jnp.sum(found, axis=0, keepdims=True) + slot_total
    load_table = pltpu.make_async_copy(table, slot_of, load_sem.at[7])
    load_table.start()

    loads[3].wait()
    turned = feats[...].astype(f32).T.astype(bf16)
    for h in range(PARTS):
        feat_all[h, i] = turned[h * piece:(h + 1) * piece]

    pl.semaphore_wait(barrier, len(peers))

    feat_copies = {}
    for h in range(PARTS):
        for d in range(rows - 1, 0, -1):
            k = h * (rows - 1) + d - 1
            feat_copies[h, d] = send(feat_all.at[h, i], feat_all.at[h, i], feat_s.at[k], feat_r.at[k], row_peer(d))

    load_table.wait()
    loads[4].wait()

    def place(r, carry):
        at = pl.ds(pl.multiple_of(r * tile, tile), tile)
        for c in range(col_tiles):
            dense[at, c * tile:(c + 1) * tile] = slots[slot_of[0, r * col_tiles + c]]
        return carry

    lax.fori_loop(0, row_tiles, place, 0)

    def block_at(index):
        if isinstance(index, int):
            return pl.ds(index * block, block)
        return pl.ds(pl.multiple_of(index * block, block), block)

    def lines(h):
        return pl.ds(h * piece, piece)

    def forward_term(h, dest, source):
        return dot_nt(feat_all[h, source], dense[block_at(dest), block_at(source)])

    own_turned = jnp.concatenate([feat_all[h, i] for h in range(PARTS)], axis=0)

    def add_own(dest):
        part[dest] = dot_nt(own_turned, dense[block_at(dest), block_at(i)])

    each(cols, add_own)

    loads[5].wait()
    loads[6].wait()
    weight_t[...] = weight[...].astype(f32).T.astype(bf16)
    cot_t[...] = cot[...].astype(f32).T

    def add_sources(h):
        for d in range(1, rows - 1):
            feat_copies[h, d].wait_recv()
            source = row_at(d)

            def add_source(dest):
                part[dest, lines(h)] += forward_term(h, dest, source)

            each(cols, add_source)

    order = list(range(chips - 1, -1, -1))
    pair_copies = {}

    def last_source(h):
        feat_copies[h, rows - 1].wait_recv()
        source = row_at(rows - 1)
        for d in order:
            dest = 2 * chip_at(d) + other
            pair_send[h, d] = (part[dest, lines(h)] + forward_term(h, dest, source)).astype(bf16)
        pair_copies[h] = send(pair_send.at[h], pair_recv.at[h], pair_s.at[h], pair_r.at[h], partner)
        for d in order:
            dest = 2 * chip_at(d) + core
            part[dest, lines(h)] += forward_term(h, dest, source)

    hop_copies = {}

    def send_hops(h):
        pair_copies[h].wait_recv()
        for d in order:
            mine = part[2 * chip_at(d) + core, lines(h)] + pair_recv[h, d].astype(f32)
            if d:
                k = h * (chips - 1) + d - 1
                hop_send[h, d - 1] = mine.astype(bf16)
                hop_copies[h, d] = send(hop_send.at[h, d - 1], hop_recv.at[h, d - 1], hop_s.at[k], hop_r.at[k],
                                        chip_peer(d))
            else:
                own_sum[h] = mine

    add_sources(0)
    last_source(0)
    for h in range(1, PARTS):
        add_sources(h)
        send_hops(h - 1)
        last_source(h)
    send_hops(PARTS - 1)

    mixed = []
    for h in range(PARTS):
        total = own_sum[h]
        for d in range(1, chips):
            hop_copies[h, d].wait_recv()
            total = total + hop_recv[h, d - 1].astype(f32)
        mixed.append(total)
    high, low = split_high_low(jnp.concatenate(mixed, axis=0))
    summed = dot_nn(weight_t[...], high) + dot_nn(weight_t[...], low)
    gate = 1.0 / (1.0 + jnp.exp(-summed))
    slope = gate * (1.0 + summed * (1.0 - gate))
    grad = (cot_t[...] * slope).astype(bf16)
    back = dot_nn(weight[...], grad).astype(bf16)
    for h in range(PARTS):
        grad_all[j, h] = back[h * piece:(h + 1) * piece]
    gz_copies = {}
    for h in range(PARTS):
        for d in order[:-1]:
            k = h * (chips - 1) + d - 1
            gz_copies[h, d] = send(grad_all.at[j, h], grad_all.at[j, h], gz_s.at[k], gz_r.at[k], chip_peer(d))
    gp_copy = send(grad_all.at[j], grad_all.at[j], gp_s.at[0], gp_r.at[0], partner)

    scale = float(rows * cols * block) ** -0.5
    w_term[...] = (dot_nt(high, grad) + dot_nt(low, grad)) * scale
    quarter = width // rows
    half = quarter // 2

    def quarter_at(index):
        return pl.ds(pl.multiple_of(index * quarter, quarter), quarter)

    w1_copies = []
    for d in range(1, rows):
        w1_copies.append(send(w_term.at[quarter_at(row_at(d))], w_row.at[d - 1], w1_s.at[d - 1], w1_r.at[d - 1],
                              row_peer(d)))

    out[...] = (summed * gate).T.astype(out.dtype)

    def add_whole(source, first):
        grads = jnp.concatenate([grad_all[source, h] for h in range(PARTS)], axis=0)
        for r in range(rows):
            term = dot_nn(grads, dense[block_at(source), r * block:(r + 1) * block])
            if first:
                acc[r] = term
            else:
                acc[r] += term

    def add_part(source, h):
        for r in range(rows):
            acc[r, lines(h)] += dot_nn(grad_all[source, h], dense[block_at(source), r * block:(r + 1) * block])

    add_whole(j, True)
    gp_copy.wait_recv()
    add_whole(2 * q + other, False)

    gf_copies = {}

    def arrive(h, d):
        gz_copies[h, d].wait_recv()
        source = 2 * chip_at(d) + core
        k = h * (chips - 1) + d - 1
        gf_copies[h, d] = send(grad_all.at[source, h], grad_all.at[source, h], gf_s.at[k], gf_r.at[k], partner)
        add_part(source, h)

    def passed(h, d):
        gf_copies[h, d].wait_recv()
        add_part(2 * chip_at(d) + other, h)

    row_copies = {}

    def send_rows(h):
        for d in range(rows - 1, 0, -1):
            k = h * (rows - 1) + d - 1
            row_send[h, d - 1] = acc[row_at(d), lines(h)].astype(bf16)
            row_copies[h, d] = send(row_send.at[h, d - 1], row_recv.at[h, d - 1], row_s.at[k], row_r.at[k],
                                    row_peer(d))

    w2_copies = []
    w3_copies = []

    def second_weight_step():
        total = w_term[quarter_at(i)]
        for d, copy in enumerate(w1_copies):
            copy.wait_recv()
            total = total + w_row[d]
        w_quarter[...] = total
        w2_copies.append(send(w_quarter.at[pl.ds(pl.multiple_of(other * half, half), half)], w_pair, w2_s.at[0],
                              w2_r.at[0], partner))

    def third_weight_step():
        w2_copies[0].wait_recv()
        w_hop[q] = w_quarter[pl.ds(pl.multiple_of(core * half, half), half)] + w_pair[...]
        for d in range(1, chips):
            w3_copies.append(send(w_hop.at[q], w_hop.at[q], w3_s.at[d - 1], w3_r.at[d - 1], chip_peer(d)))

    arrivals = [(h, d) for h in range(PARTS) for d in range(1, chips)]
    for at, (h, d) in enumerate(arrivals):
        arrive(h, d)
        if at == 1:
            second_weight_step()
        if at == chips - 1:
            third_weight_step()
        if at:
            before = arrivals[at - 1]
            passed(*before)
            if before[1] == chips - 1:
                send_rows(before[0])
    passed(*arrivals[-1])
    send_rows(PARTS - 1)

    for copy in w3_copies:
        copy.wait_recv()
    total = w_hop[0]
    for k in range(1, chips):
        total = total + w_hop[k]
    w_all[core, i] = total
    w4_copies = []
    for d in range(1, rows):
        w4_copies.append(send(w_all.at[core, i], w_all.at[core, i], w4_s.at[d - 1], w4_r.at[d - 1], row_peer(d)))

    finals = []
    for h in range(PARTS):
        final = acc[i, lines(h)]
        for d in range(1, rows):
            row_copies[h, d].wait_recv()
            final = final + row_recv[h, d - 1].astype(f32)
        finals.append(final)
    grad_feat[...] = jnp.concatenate(finals, axis=0).T.astype(grad_feat.dtype)
    for copy in w4_copies:
        copy.wait_recv()
    w5_copy = send(w_all.at[core], w_all.at[core], w5_s.at[0], w5_r.at[0], partner)
    w5_copy.wait_recv()
    for r in range(rows):
        for c in range(2):
            at = (2 * r + c) * half
            grad_weight[at:at + half] = w_all[c, r]
    for copy in started:
        copy.wait_send()


def local(features, weight, cotangent, tile_values, tile_rows, tile_cols, tile_counts):
    rows = lax.axis_size("row")
    cols = lax.axis_size("col")
    chips = cols // 2
    block, width = features.shape
    hidden = weight.shape[1]
    slot_total, tile = tile_values.shape[2], tile_values.shape[3]
    row_tiles = cols * block // tile
    col_tiles = rows * block // tile
    cell_total = row_tiles * col_tiles
    half = width // rows // 2
    piece = width // PARTS
    bf16, f32, i32 = jnp.bfloat16, jnp.float32, jnp.int32
    dma = pltpu.SemaphoreType.DMA
    v = pltpu.VMEM
    sizes = (block, tile, row_tiles, col_tiles, slot_total)
    scratch = [
        v((1, 1), i32),
        v((1, slot_total), i32),
        v((1, slot_total), i32),
        v((block, width), bf16),
        v((width, hidden), bf16),
        v((block, hidden), bf16),
        v((1, pl.cdiv(slot_total, 128) * 128), i32),
        v((1, cell_total), i32),
        pltpu.SMEM((1, cell_total), i32),
        v((slot_total + 1, tile, tile), bf16),
        v((row_tiles * tile, col_tiles * tile), bf16),
        v((hidden, width), bf16),
        v((hidden, block), f32),
        v((PARTS, rows, piece, block), bf16),
        v((cols, width, block), f32),
        v((PARTS, chips, piece, block), bf16),
        v((PARTS, chips, piece, block), bf16),
        v((PARTS, piece, block), f32),
        v((PARTS, chips - 1, piece, block), bf16),
        v((PARTS, chips - 1, piece, block), bf16),
        v((cols, PARTS, piece, block), bf16),
        v((rows, width, block), f32),
        v((PARTS, rows - 1, piece, block), bf16),
        v((PARTS, rows - 1, piece, block), bf16),
        v((width, hidden), f32),
        v((rows - 1, 2 * half, hidden), f32),
        v((2 * half, hidden), f32),
        v((half, hidden), f32),
        v((chips, half, hidden), f32),
        v((2, rows, half, hidden), f32),
        dma((8,)),
    ]
    for count in (PARTS * (rows - 1), PARTS, PARTS * (chips - 1), 1, PARTS * (chips - 1), PARTS * (chips - 1),
                  PARTS * (rows - 1), rows - 1, 1, chips - 1, rows - 1, 1):
        scratch += [dma((count,)), dma((count,))]
    vmem = pl.BlockSpec(memory_space=pltpu.VMEM)
    hbm = pl.BlockSpec(memory_space=pltpu.HBM)
    shapes = (((block, hidden), bf16), ((block, width), bf16), ((width, hidden), f32))
    values = pl.pallas_call(
        functools.partial(kernel, rows, cols, sizes),
        out_shape=[pltpu.VMEM(*shape) for shape in shapes],
        in_specs=[hbm] * 7,
        out_specs=[vmem] * 3,
        scratch_shapes=scratch,
        compiler_params=pltpu.CompilerParams(
            collective_id=0, has_side_effects=True, vmem_limit_bytes=56 * 2**20),
    )(tile_counts, tile_rows[0], tile_cols[0], features, weight, cotangent, tile_values[0, 0])
    values = [pltpu.with_memory_space_constraint(value, pltpu.VMEM) for value in values]
    return pl.pallas_call(
        finish,
        out_shape=[jax.ShapeDtypeStruct(*shape) for shape in shapes],
        in_specs=[vmem] * 3,
        out_specs=[hbm] * 3,
        scratch_shapes=[dma((3,))],
    )(*values)


def solution(mesh):
    placed = (
        P(("row", "col"), None),
        P(),
        P(("row", "col"), None),
        P("row", "col", None, None, None),
        P("row", "col", None),
        P("row", "col", None),
        P("row", "col"),
    )
    return jax.shard_map(
        local,
        mesh=mesh,
        in_specs=placed,
        out_specs=(P(("row", "col"), None), P(("row", "col"), None), P()),
        check_vma=False,
    )
```

time: 42.2 us -> 37 us (0.88)
  Pallas kernels: 40.8 us -> 35.6 us
    pallas_call x2, Pallas kernels: 40.8 us -> 35.6 us  [the longest x1 34.8 us: local(): pl.pallas_call(functools.partial(kernel, rows, cols, sizes), out_shape=[p...]
where the time goes in v1:
time: 37 us; the launch traced here: 36.9 us
  Pallas kernels  35.6 us (96%)
  between operations  1.29 us (3%)
    pallas_call x1, Pallas kernels, local(): pl.pallas_call(functools.partial(kernel, rows, cols, sizes), out_shape=[p...  34.8 us
    pallas_call x1, Pallas kernels, local(): pl.pallas_call(finish, out_shape=[jax.ShapeDtypeStruct(*shape) for shape...  0.75 us

profile of v1, /device:TPU:0, one launch (start us, length us, event | category | flops | bytes accessed | tf_op | source)
XLA Modules:
  0.0 36.9 jit_solution(2329989933626792144)
XLA Ops:
  1.3 34.8 %shard_map.94 = (bf16[256,256]{1,0:T(8,128)(2,1)S(1)}, bf16[256,128]{1,0:T(8,128)(2,1)S(1)}, f32[128,256]{1,0:T(8,128)S(1)}) custom-call(s32[1,1]{1,0:T(1,128)S(6)} %copy.10.live_hbm, s32[1,96]{1,0:T(1,128)} %bitcast.4, s32[1,96]{1,0:T(1,128)} %bitcast.5, bf16[256,128]{1,0:T(8,128)(2,1)} %feats_hbm.1, bf16[128,256]{1,0:T(8,128)(2,1)} %weight_hbm.1, ...), custom_call_target="tpu_custom_call" | custom-call | tf_op jit(solution)/shard_map/pallas_call | solution.py:412
  36.1 0.7 %shard_map.95 = (bf16[256,256]{1,0:T(8,128)(2,1)}, bf16[256,128]{1,0:T(8,128)(2,1)}, f32[128,256]{1,0:T(8,128)}) custom-call(bf16[256,256]{1,0:T(8,128)(2,1)S(1)} %get-tuple-element.6.refs_0_, bf16[256,128]{1,0:T(8,128)(2,1)S(1)} %get-tuple-element.7.refs_1_, f32[128,256]{1,0:T(8,128)S(1)} %get-tuple-element.8.refs_2_), custom_call_target="tpu_custom_call" | custom-call | tf_op jit(solution)/shard_map/pallas_call | solution.py:422
